TPU v7x, 512 devices: a whole 4x4x16 slice. The times are simulated.
512 devices in a mesh: gz: 128 (over z, y, core), row: 4 (over x).
Axes of the slice: x: 4, y: 4, z: 16, core: 2. Of those that a mesh axis runs over, the one named last changes fastest.
Arguments:
- tokens: bfloat16 [262144, 384], P(('gz', 'row')), may hold values from -6 to 6
- key_blocks: int32 [4096, 20], P(('gz', 'row')), may hold values from 0 to 4095, as said below
- counts: int32 [128], replicated, may hold values from 8 to 32, as said below
- norm_gain: float32 [384], replicated, may hold values from 0.1 to 1.9
- qkv_weight: bfloat16 [384, 1152], replicated, may hold values from -1 to 1
- out_weight: bfloat16 [384, 384], replicated, may hold values from -0.3125 to 0.3125
- mlp_gain: float32 [384], replicated, may hold values from 0.1 to 1.9
- up_weight: bfloat16 [384, 1536], replicated, may hold values from -0.3125 to 0.3125
- down_weight: bfloat16 [1536, 384], replicated, may hold values from -0.15625 to 0.15625
Outputs:
- block_out: bfloat16 [262144, 384], P(('gz', 'row'))
Inputs may be any that keep to these rules, and one draw needn't show every extreme that they name: `key_blocks`: entries 0 to 3 of a query block's list name live blocks of the query's own slab (repeats possible). The other 16 entries name blocks with the same row group as the query block (id % 32 // 8 equal), in any slab; over the blocks of one device each slab is named by exactly 1 such entries. `counts`: one slab is full in every draw.
All inputs are finite; a program needn't handle non-finite values.
Results may differ from a plain program's by a relative error of at most 0.01.
Values may be sent and summed in bfloat16 or wider, within the bound.
A program may use at most 128 MiB of HBM per device.

v0:
```python
import jax
import jax.numpy as jnp
from jax import lax
from jax.sharding import PartitionSpec as P

H = 12
NNEAR = 4
NFAR = 16


def rms_norm(values, gain):
    mean_sq = jnp.mean(values * values, axis=-1, keepdims=True)
    return values * lax.rsqrt(mean_sq + 1e-05) * gain


def attend(query_block, key_values, live_blocks):
    model_width = query_block.shape[1]
    head_size = model_width // H
    keys = key_values[:, :, :model_width].reshape(-1, H, head_size)
    values = key_values[:, :, model_width:].reshape(-1, H, head_size)
    heads = query_block.reshape(-1, H, head_size)
    scores = jnp.einsum("qhd,khd->hqk", heads, keys, preferred_element_type=jnp.float32) / jnp.sqrt(
        jnp.float32(head_size)
    )
    key_live = jnp.repeat(live_blocks, key_values.shape[1])
    scores = jnp.where(key_live[None, None, :], scores, jnp.float32(-1e30))
    top = jnp.max(scores, axis=-1, keepdims=True)
    weights = jnp.exp(scores - top)
    total = jnp.sum(weights, axis=-1)
    mixed = jnp.einsum(
        "hqk,khd->qhd", weights.astype(jnp.bfloat16), values, preferred_element_type=jnp.float32
    )
    mixed = mixed / jnp.transpose(total)[:, :, None]
    return mixed.reshape(-1, model_width).astype(jnp.bfloat16)


def body(
    tokens, key_blocks, counts, norm_gain, qkv_weight, out_weight, mlp_gain, up_weight, down_weight
):
    model_width = tokens.shape[1]
    own_blocks = key_blocks.shape[0]
    block_len = tokens.shape[0] // own_blocks
    slabs_n = lax.axis_size("gz")
    slab_blocks = own_blocks * lax.axis_size("row")
    inputs = tokens.astype(jnp.float32)
    normed = rms_norm(inputs, norm_gain).astype(jnp.bfloat16)
    projected = jnp.dot(normed, qkv_weight, preferred_element_type=jnp.float32).astype(jnp.bfloat16)
    queries = projected[:, :model_width].reshape(own_blocks, block_len, model_width)
    kv_own = projected[:, model_width:].reshape(own_blocks, block_len, 2 * model_width)
    slab_kv = lax.all_gather(kv_own, "row", axis=0, tiled=True)
    owner_slab = key_blocks // slab_blocks
    within = key_blocks % slab_blocks
    slab_table = jnp.arange(slabs_n, dtype=jnp.int32)
    slab_count = jnp.sum(jnp.where(owner_slab[:, :, None] == slab_table, counts, 0), axis=-1)
    live = within < slab_count
    near_rows = within[:, :NNEAR]
    far_owner = owner_slab[:, NNEAR:].reshape(-1)
    far_local = (key_blocks[:, NNEAR:] % own_blocks).reshape(-1)
    request_count = far_owner.shape[0]
    per_owner = request_count // slabs_n
    slab_hits = (far_owner[:, None] == slab_table[None, :]).astype(jnp.int32)
    slot_rank = jnp.sum((jnp.cumsum(slab_hits, axis=0) - 1) * slab_hits, axis=1)
    far_slot = far_owner * per_owner + slot_rank
    slot_hits = far_slot[:, None] == jnp.arange(request_count, dtype=jnp.int32)[None, :]
    request = jnp.sum(jnp.where(slot_hits, far_local[:, None], 0), axis=0)
    wanted = lax.all_to_all(
        request.reshape(slabs_n, per_owner), "gz", split_axis=0, concat_axis=0, tiled=True
    ).reshape(-1)
    kv_sent = kv_own[wanted].reshape(slabs_n, per_owner, block_len, 2 * model_width)
    far_kv = lax.all_to_all(kv_sent, "gz", split_axis=0, concat_axis=0, tiled=True).reshape(
        request_count, block_len, 2 * model_width
    )
    far_slots = far_slot.reshape(own_blocks, NFAR)

    def one_block(packed):
        query_block, near_row, slot_row, live_blocks = packed
        gathered = jnp.concatenate([slab_kv[near_row], far_kv[slot_row]], axis=0)
        return attend(query_block, gathered, live_blocks)

    attended = lax.map(one_block, (queries, near_rows, far_slots, live)).reshape(-1, model_width)
    residual = (inputs + jnp.dot(attended, out_weight, preferred_element_type=jnp.float32)).astype(
        jnp.bfloat16
    )
    normed_two = rms_norm(residual.astype(jnp.float32), mlp_gain).astype(jnp.bfloat16)
    hidden = jax.nn.gelu(jnp.dot(normed_two, up_weight, preferred_element_type=jnp.float32)).astype(
        jnp.bfloat16
    )
    result = residual.astype(jnp.float32) + jnp.dot(
        hidden, down_weight, preferred_element_type=jnp.float32
    )
    return result.astype(jnp.bfloat16)


def solution(mesh):
    return jax.shard_map(
        body,
        mesh=mesh,
        in_specs=(
            P(("gz", "row"), None),
            P(("gz", "row"), None),
            P(),
            P(),
            P(),
            P(),
            P(),
            P(),
            P(),
        ),
        out_specs=P(("gz", "row"), None),
        check_vma=False,
    )
```

profile of v0, /device:TPU:1, one launch (start us, length us, event | category | flops | bytes accessed | tf_op | source)
XLA Modules:
  0.0 899.0 jit_solution(1121670228715320951)
XLA Ops:
  9.8 20.6 %all-to-all-start = ((s32[128,1,1]{2,1,0:T(1,128)}), s32[128,1,1]{2,1,0:T(1,128)S(1)}, u32[]{:S(2)}, u32[]{:S(2)}) async-start(s32[128,1,1]{2,1,0:T(1,128)} %copy.50), calls=%async_computation | async-start | bytes 131072 | tf_op jit(solution)/shard_map/all_to_all | solution.py:66
  34.5 10.7 %all-to-all-done = s32[128,1,1]{2,1,0:T(1,128)S(1)} async-done(((s32[128,1,1]{2,1,0:T(1,128)}), s32[128,1,1]{2,1,0:T(1,128)S(1)}, u32[]{:S(2)}, u32[]{:S(2)}) %all-to-all-start) | async-done | bytes 544 | tf_op jit(solution)/shard_map/all_to_all | solution.py:66
  47.5 8.3 gather_fusion.2
  55.8 7.0 all-to-all-start.1
  67.0 46.9 %all-gather.2.cloned.1.call-done = bf16[32,64,768]{2,1,0:T(8,128)(2,1)} async-done(((bf16[8,64,768]{2,1,0:T(8,128)(2,1)}), bf16[32,64,768]{2,1,0:T(8,128)(2,1)}) %all-gather.2.cloned.1.call-update) | async-done | bytes 3145744 | tf_op jit(solution)/shard_map/all_gather | solution.py:50
  113.9 493.9 %all-to-all-done.1 = bf16[128,1,64,768]{3,2,1,0:T(8,128)(2,1)} async-done(((bf16[128,1,64,768]{3,2,1,0:T(8,128)(2,1)}), bf16[128,1,64,768]{3,2,1,0:T(8,128)(2,1)}, u32[]{:S(2)}, u32[]{:S(2)}) %all-to-all-start.1) | async-done | bytes 12582944 | tf_op jit(solution)/shard_map/all_to_all | solution.py:70
  607.9 278.2 %while.10 = (s32[]{:T(128)}, bf16[8,64,384]{2,1,0:T(8,128)(2,1)}, s32[8,4]{1,0:T(8,128)}, bf16[32,64,768]{2,1,0:T(8,128)(2,1)}, s32[8,16]{1,0:T(8,128)}, /*index...) while((s32[]{:T(128)}, bf16[8,64,384]{2,1,0:T(8,128)(2,1)}, ...), condition=%wide.region_8.9_spmd, body=%wide.region_5.8_spmd.sunk | while | flops 132760128 | bytes 49673220 | solution.py:80
  609.2 2.5 gather_fusion
  612.5 5.2 gather_fusion.1
  619.0 3.0 fusion.76
  622.0 2.8 copy.69
  624.8 2.4 reshape.201
  633.6 2.8 copy.67
  638.7 3.1 fusion.79
  644.0 2.5 gather_fusion
  647.3 5.2 gather_fusion.1
  653.8 3.0 fusion.76
  656.8 2.8 copy.69
  659.6 2.4 reshape.201
  668.4 2.8 copy.67
  673.5 3.1 fusion.79
  678.8 2.5 gather_fusion
  682.0 5.2 gather_fusion.1
  688.6 3.0 fusion.76
  691.6 2.8 copy.69
  694.3 2.4 reshape.201
  703.1 2.8 copy.67
  708.3 3.1 fusion.79
  713.5 2.5 gather_fusion
  716.8 5.2 gather_fusion.1
  723.3 3.0 fusion.76
  726.3 2.8 copy.69
  729.1 2.4 reshape.201
  737.9 2.8 copy.67
  743.1 3.1 fusion.79
  748.3 2.5 gather_fusion
  751.6 5.2 gather_fusion.1
  758.1 3.0 fusion.76
  761.1 2.8 copy.69
  763.9 2.4 reshape.201
  772.7 2.8 copy.67
  777.8 3.1 fusion.79
  783.1 2.5 gather_fusion
  786.4 5.2 gather_fusion.1
  792.9 3.0 fusion.76
  795.9 2.8 copy.69
  798.7 2.4 reshape.201
  807.5 2.8 copy.67
  812.6 3.1 fusion.79
  817.9 2.5 gather_fusion
  821.1 5.2 gather_fusion.1
  827.7 3.0 fusion.76
  830.7 2.8 copy.69
  833.4 2.4 reshape.201
  842.2 2.8 copy.67
  847.4 3.1 fusion.79
  852.7 2.5 gather_fusion
  855.9 5.2 gather_fusion.1
  862.4 3.0 fusion.76
  865.4 2.8 copy.69
  868.2 2.4 reshape.201
  877.0 2.8 copy.67
  882.2 3.1 fusion.79
  887.7 3.5 fusion.29
  (181 shorter events, 120.1 us)
Async XLA Ops:
  6.5 881.2 %copy-start = (bf16[1536,384]{1,0:T(8,128)(2,1)S(1)}, bf16[1536,384]{1,0:T(8,128)(2,1)}, u32[]{:S(2)}) copy-start(bf16[1536,384]{1,0:T(8,128)(2,1)} %param.19) | copy-start | bytes 3538948
  9.8 35.4 %all-to-all-start = ((s32[128,1,1]{2,1,0:T(1,128)}), s32[128,1,1]{2,1,0:T(1,128)S(1)}, u32[]{:S(2)}, u32[]{:S(2)}) async-start(s32[128,1,1]{2,1,0:T(1,128)} %copy.50), calls=%async_computation | async-start | bytes 131072 | tf_op jit(solution)/shard_map/all_to_all | solution.py:66
  31.5 0.8 copy-start.3
  34.5 21.4 %copy-start.2 = (bf16[512,768]{1,0:T(8,128)(2,1)}, bf16[512,768]{1,0:T(8,128)(2,1)S(1)}, u32[]{:S(2)}) copy-start(bf16[512,768]{1,0:T(8,128)(2,1)S(1)} %slice.35) | copy-start | bytes 2359300
  55.8 9.4 %copy-start.4 = (s32[128]{0:T(128)S(1)}, s32[128]{0:T(128)}, u32[]{:S(2)}) copy-start(s32[128]{0:T(128)} %param.13) | copy-start | bytes 1540
  55.8 552.0 %all-to-all-start.1 = ((bf16[128,1,64,768]{3,2,1,0:T(8,128)(2,1)}), bf16[128,1,64,768]{3,2,1,0:T(8,128)(2,1)}, u32[]{:S(2)}, u32[]{:S(2)}) async-start(bf16[128,1,64,768]{3,2,1,0:T(8,128)(2,1)} %bitcast.77), calls=%async_computation.1 | async-start | bytes 25165824 | tf_op jit(solution)/shard_map/all_to_all | solution.py:70
  62.8 51.1 %all-gather.2.cloned.1.call-start = ((), (), s32[]{:S(2)}) async-start(), calls=%async_computation.2 | async-start | bytes 3932160 | tf_op jit(solution)/shard_map/all_gather | solution.py:50
  631.0 1.9 copy-start.1
  665.7 1.9 copy-start.1
  700.5 1.9 copy-start.1
  735.3 1.9 copy-start.1
  770.1 1.9 copy-start.1
  804.8 1.9 copy-start.1
  839.6 1.9 copy-start.1
  874.4 1.9 copy-start.1
Sparse Core Ops, SparseCore 0:
  65.8 48.1 all-gather.1
where the time goes:
time: 903 us; the launch traced here: 899 us
  waiting for transfers between devices  552 us (61%)
  local copies, waits for them, and re-layouts  236 us (26%)
  matrix products  48.5 us (5%)
  starting transfers between devices  27.8 us (3%)
  other arithmetic  21.2 us (2%)
  between operations  13.5 us (1%)
    all_to_all x1, waiting for transfers between devices, body(): lax.all_to_all(kv_sent, 'gz', split_axis=0, concat_axis=0, tiled=True)  494 us
    gather x16, local copies, waits for them, and re-layouts, one_block(): gathered = jnp.concatenate([slab_kv[near_row], far_kv[slot_row]], axis=0)  61.5 us
    all_gather x1, waiting for transfers between devices, body(): slab_kv = lax.all_gather(kv_own, 'row', axis=0, tiled=True)  46.9 us
    slice x16, local copies, waits for them, and re-layouts, attend(): keys = key_values[:, :, :model_width].reshape(-1, H, head_size)  46.1 us
    dot_general x8, matrix products, attend(): jnp.einsum('hqk,khd->qhd', weights.astype(jnp.bfloat16), values, preferre...  25.1 us
    slice x8, local copies, waits for them, and re-layouts, attend(): values = key_values[:, :, model_width:].reshape(-1, H, head_size)  22.3 us
    while x24, local copies, waits for them, and re-layouts  21.4 us
    all_to_all x1, starting transfers between devices, body(): lax.all_to_all(request.reshape(slabs_n, per_owner), 'gz', split_axis=0, c...  20.6 us
  transfers between devices with their start and end apart: 3, of which 3 were waited for; matrix products, arithmetic and copies ran while one was open for 1% of the time, Pallas kernels for 0%

commit v1 on v0

v1 whole, which is shorter than its diff:
```python
import functools

import jax
import jax.numpy as jnp
from jax import lax
from jax.experimental import pallas as pl
from jax.experimental.pallas import tpu as pltpu
from jax.sharding import PartitionSpec as P

H = 12
NNEAR = 4
NFAR = 16
NZ = 16
NJ = 8
NX = 4
MESH = pl.DeviceIdType.MESH


def rms_norm(values, gain):
    mean_sq = jnp.mean(values * values, axis=-1, keepdims=True)
    return values * lax.rsqrt(mean_sq + 1e-05) * gain


def comm_kernel(tok_ref, gain_ref, req_ref, far_ref, near_ref, nrm_ref, *scratch):
    fwd = scratch[0:7]
    bwd = scratch[7:14]
    opp = scratch[14]
    send_buf, req_in, req_s = scratch[15:18]
    fs_sem, fr_sem, bs_sem, br_sem, ys_sem, yr_sem, xs_sem, xr_sem, qs_sem, qr_sem, loc_sem = scratch[18:]
    gz = lax.axis_index("gz")
    x = lax.axis_index("row")
    z = gz // NJ
    j = lax.rem(gz, NJ)
    z_up = lax.rem(z + 1, NZ) * NJ + j
    z_down = lax.rem(z + NZ - 1, NZ) * NJ + j

    def plane(o):
        return z * NJ + lax.rem(j + o, NJ)

    def along(o):
        return lax.rem(x + o, NX)

    barrier = pltpu.get_barrier_semaphore()
    for peer in (z_up, z_down):
        pl.semaphore_signal(barrier, inc=1, device_id=(peer, x), device_id_type=MESH)
    for o in range(1, NJ):
        pl.semaphore_signal(barrier, inc=1, device_id=(plane(o), x), device_id_type=MESH)
    for o in range(1, NX):
        pl.semaphore_signal(barrier, inc=1, device_id=(gz, along(o)), device_id_type=MESH)
    pl.semaphore_wait(barrier, 2 + NJ - 1 + NX - 1)

    def req_copy(o):
        return pltpu.make_async_remote_copy(
            src_ref=req_ref.at[NJ - o], dst_ref=req_in.at[o],
            send_sem=qs_sem.at[o], recv_sem=qr_sem.at[o],
            device_id=(plane(NJ - o), x), device_id_type=MESH)

    for o in range(1, NJ):
        req_copy(o).start()
    req_in[0] = req_ref[0]

    values = tok_ref[...].astype(jnp.float32)
    nrm_ref[...] = rms_norm(values, gain_ref[...]).astype(jnp.bfloat16)

    half = NJ // 2

    def ring(k, h, forward):
        slots = fwd if forward else bwd
        src = nrm_ref if k == 1 else slots[k - 2]
        dst = opp if k == 8 else slots[k - 1]
        part = pl.ds(h * half, half)
        return pltpu.make_async_remote_copy(
            src_ref=src.at[part], dst_ref=dst.at[part],
            send_sem=(fs_sem if forward else bs_sem).at[k, h],
            recv_sem=(fr_sem if forward else br_sem).at[k, h],
            device_id=(z_up if forward else z_down, x), device_id_type=MESH)

    def near_copy(o):
        return pltpu.make_async_remote_copy(
            src_ref=nrm_ref, dst_ref=near_ref.at[o],
            send_sem=xs_sem.at[o], recv_sem=xr_sem.at[o],
            device_id=(gz, along(o)), device_id_type=MESH)

    for h in range(2):
        ring(1, h, True).start()
        ring(1, h, False).start()
    for o in range(1, NX):
        near_copy(o).start()
    near_ref[0] = nrm_ref[...]
    for o in range(1, NJ):
        req_copy(o).wait_recv()
    copy = pltpu.make_async_copy(req_in, req_s, loc_sem)
    copy.start()
    copy.wait()

    def plane_copy(k, o):
        first, count = (0, 1) if k == 0 else (15, 1) if k == 8 else (2 * k - 1, 2)
        part = pl.ds(first, count)
        return pltpu.make_async_remote_copy(
            src_ref=send_buf.at[o, part], dst_ref=far_ref.at[o, part],
            send_sem=ys_sem.at[k, o], recv_sem=yr_sem.at[k, o],
            device_id=(plane(o), x), device_id_type=MESH)

    def forward_plane(k, held):
        for p, ref in held:
            far_ref[0, p] = ref[req_s[0, 0, p]]

        def one(o, carry):
            for p, ref in held:
                send_buf[o, p] = ref[req_s[o, 0, p]]
            plane_copy(k, o).start()
            return carry

        lax.fori_loop(1, NJ, one, 0)

    forward_plane(0, [(0, nrm_ref)])
    for k in range(1, 8):
        for h in range(2):
            ring(k, h, True).wait_recv()
            if k < 7 or h == 0:
                ring(k + 1, h, True).start()
            ring(k, h, False).wait_recv()
            if k < 7 or h == 1:
                ring(k + 1, h, False).start()
        forward_plane(k, [(2 * k - 1, bwd[k - 1]), (2 * k, fwd[k - 1])])
    ring(8, 0, True).wait_recv()
    ring(8, 1, False).wait_recv()
    forward_plane(8, [(15, opp)])

    for o in range(1, NX):
        near_copy(o).wait_recv()
    for k in range(9):
        def arrive(o, carry, k=k):
            plane_copy(k, o).wait_recv()
            return carry
        lax.fori_loop(1, NJ, arrive, 0)
    for k in range(1, 9):
        for h in range(2):
            if k < 8 or h == 0:
                ring(k, h, True).wait_send()
            if k < 8 or h == 1:
                ring(k, h, False).wait_send()
    for o in range(1, NX):
        near_copy(o).wait_send()
    for o in range(1, NJ):
        req_copy(o).wait_send()
    for k in range(9):
        def left(o, carry, k=k):
            plane_copy(k, o).wait_send()
            return carry
        lax.fori_loop(1, NJ, left, 0)


def exchange(tokens, gain, requests):
    blocks, length, width = tokens.shape
    vmem = pl.BlockSpec(memory_space=pltpu.VMEM)
    block = (blocks, length, width)
    bf16 = jnp.bfloat16
    dma = pltpu.SemaphoreType.DMA
    return pl.pallas_call(
        comm_kernel,
        name="exchange",
        out_shape=(
            jax.ShapeDtypeStruct((NJ, NZ, length, width), bf16),
            jax.ShapeDtypeStruct((NX, blocks, length, width), bf16),
            jax.ShapeDtypeStruct(block, bf16),
        ),
        in_specs=[vmem] * 3,
        out_specs=(vmem,) * 3,
        scratch_shapes=[pltpu.VMEM(block, bf16)] * 15
        + [
            pltpu.VMEM((NJ, NZ, length, width), bf16),
            pltpu.VMEM((NJ, 1, 128), jnp.int32),
            pltpu.SMEM((NJ, 1, 128), jnp.int32),
            dma((9, 2)), dma((9, 2)), dma((9, 2)), dma((9, 2)),
            dma((9, NJ)), dma((9, NJ)),
            dma((NX,)), dma((NX,)),
            dma((NJ,)), dma((NJ,)),
            dma,
        ],
        compiler_params=pltpu.CompilerParams(
            collective_id=0, has_side_effects=True, vmem_limit_bytes=60 << 20
        ),
    )(tokens, gain, requests)


def block_kernel(
    pos_ref, live_ref, tok_ref, nrm_ref, far_ref, near_ref, wq_ref, wk_ref, wv_ref, wo_ref,
    gain_ref, up_ref, down_ref, out_ref, qp_ref, stage_ref, mixed_ref, att_ref
):
    tokens, width = tok_ref.shape
    own = tokens // 64
    f32, bf16 = jnp.float32, jnp.bfloat16
    head = width // H
    scale = 1.4426950408889634 / (head ** 0.5)
    wide = qp_ref.shape[2]
    lane = lax.broadcasted_iota(jnp.int32, (64, wide - width), 1)

    queries = jnp.dot(nrm_ref[...], wq_ref[...], preferred_element_type=f32).astype(bf16)
    group = lax.broadcasted_iota(jnp.int32, (tokens, 128), 1) // head
    for h in range(H):
        g = h * head // 128
        cols = slice(g * 128, g * 128 + 128)
        part = jnp.where(group == h % (128 // head), queries[:, cols], jnp.zeros((), bf16))
        folded = lax.dot_general(
            part, wk_ref[:, cols], (((1,), (1,)), ((), ())), preferred_element_type=f32
        )
        folded = (folded * scale).astype(bf16)
        for b in range(own):
            qp_ref[b, h * 64:(h + 1) * 64, :width] = folded[b * 64:(b + 1) * 64]
            qp_ref[b, h * 64:(h + 1) * 64, width:] = jnp.where(lane == 1, 1.0, 0.0).astype(bf16)

    def one_block(b, carry):
        for n in range(NNEAR + NFAR):
            rows = slice(n * 64, n * 64 + 64)
            ref = near_ref if n < NNEAR else far_ref
            stage_ref[rows, :width] = ref[pos_ref[b, n]]
            bias = jnp.where(live_ref[b, n] > 0, 0.0, -1e30)
            stage_ref[rows, width:] = jnp.where(
                lane == 0, 1.0, jnp.where(lane == 1, bias, 0.0)).astype(bf16)
        rows_c = 256
        for c in range(H * 64 // rows_c):
            rows = slice(c * rows_c, (c + 1) * rows_c)
            scores = lax.dot_general(
                qp_ref[b, rows], stage_ref[...], (((1,), (1,)), ((), ())), preferred_element_type=f32
            )
            top = jnp.max(scores, axis=-1, keepdims=True)
            weights = jnp.exp2(scores - top).astype(bf16)
            mixed = jnp.dot(weights, stage_ref[...], preferred_element_type=f32)
            total = mixed[:, width:width + 1]
            result = (mixed[:, :width] / total).astype(bf16)
            for i in range(rows_c // 64):
                mixed_ref[c * (rows_c // 64) + i, pl.ds(b * 64, 64)] = result[i * 64:(i + 1) * 64]
        return carry

    lax.fori_loop(0, own, one_block, 0)

    wgroup = lax.broadcasted_iota(jnp.int32, (width, 128), 1) // head
    for g in range(width // 128):
        cols = slice(g * 128, g * 128 + 128)
        acc = jnp.zeros((tokens, 128), f32)
        for i in range(128 // head):
            part = jnp.where(wgroup == i, wv_ref[:, cols], jnp.zeros((), bf16))
            acc += jnp.dot(mixed_ref[g * (128 // head) + i], part, preferred_element_type=f32)
        att_ref[:, cols] = acc.astype(bf16)

    residual = (
        tok_ref[...].astype(f32) + jnp.dot(att_ref[...], wo_ref[...], preferred_element_type=f32)
    ).astype(bf16)
    residual = residual.astype(f32)
    second = rms_norm(residual, gain_ref[...]).astype(bf16)
    hidden = jax.nn.gelu(jnp.dot(second, up_ref[...], preferred_element_type=f32)).astype(bf16)
    result = residual + jnp.dot(hidden, down_ref[...], preferred_element_type=f32)
    out_ref[...] = result.astype(bf16)


def attention(pos, live, tokens, normed, far, near, wq, wk, wv, wo, gain, up, down):
    count, width = tokens.shape
    vmem = pl.BlockSpec(memory_space=pltpu.VMEM)
    smem = pl.BlockSpec(memory_space=pltpu.SMEM)
    bf16 = jnp.bfloat16
    return pl.pallas_call(
        block_kernel,
        name="attention",
        out_shape=jax.ShapeDtypeStruct(tokens.shape, bf16),
        in_specs=[smem] * 2 + [vmem] * 11,
        out_specs=vmem,
        scratch_shapes=[
            pltpu.VMEM((count // 64, H * 64, 512), bf16),
            pltpu.VMEM(((NNEAR + NFAR) * 64, 512), bf16),
            pltpu.VMEM((H, count, width), bf16),
            pltpu.VMEM((count, width), bf16),
        ],
        compiler_params=pltpu.CompilerParams(vmem_limit_bytes=60 << 20),
    )(pos, live, tokens, normed, far, near, wq, wk, wv, wo, gain, up, down)


def body(
    tokens, key_blocks, counts, norm_gain, qkv_weight, out_weight, mlp_gain, up_weight, down_weight
):
    width = tokens.shape[1]
    own = key_blocks.shape[0]
    length = tokens.shape[0] // own
    slabs = counts.shape[0]
    gz = lax.axis_index("gz")
    x = lax.axis_index("row")
    z, j = gz // NJ, gz % NJ
    slab_blocks = own * NX
    owner = key_blocks // slab_blocks
    within = key_blocks % slab_blocks
    table = jnp.arange(slabs, dtype=jnp.int32)
    slab_count = jnp.sum(jnp.where(owner[:, :, None] == table, counts, 0), axis=-1)
    live = (within < slab_count).astype(jnp.int32)

    place = jnp.arange(NZ, dtype=jnp.int32)
    z_off = jnp.where(place == 15, 8, jnp.where(place % 2 == 1, (place + 1) // 2, (NZ - place // 2) % NZ))
    want = ((z + z_off) % NZ)[None, :] * NJ + ((j + jnp.arange(NJ, dtype=jnp.int32)) % NJ)[:, None]
    far_owner = owner[:, NNEAR:].reshape(-1)
    far_local = (key_blocks[:, NNEAR:] % own).reshape(-1)
    requests = jnp.sum(
        jnp.where(want[:, :, None] == far_owner, far_local, 0), axis=-1)
    requests = jnp.pad(requests, ((0, 0), (0, 128 - NZ))).reshape(NJ, 1, 128)

    z_rel = (owner // NJ - z) % NZ
    order = jnp.where(z_rel == 0, 0, jnp.where(z_rel == 8, 15, jnp.where(z_rel < 8, 2 * z_rel - 1, 2 * (NZ - z_rel))))
    far_pos = ((j - owner % NJ) % NJ) * NZ + order
    near_pos = ((x - within // own) % NX) * own + within % own
    column = jnp.arange(key_blocks.shape[1])[None, :]
    pos = jnp.where(column < NNEAR, near_pos, far_pos)

    far, near, normed = exchange(
        tokens.reshape(own, length, width), norm_gain.reshape(1, 1, width), requests)
    return attention(
        pos, live, tokens, normed.reshape(-1, width), far.reshape(-1, length, width), near.reshape(-1, length, width),
        qkv_weight[:, :width], qkv_weight[:, width:2 * width], qkv_weight[:, 2 * width:],
        out_weight, mlp_gain.reshape(1, width), up_weight, down_weight)


def solution(mesh):
    return jax.shard_map(
        body,
        mesh=mesh,
        in_specs=(
            P(("gz", "row"), None),
            P(("gz", "row"), None),
            P(),
            P(),
            P(),
            P(),
            P(),
            P(),
            P(),
        ),
        out_specs=P(("gz", "row"), None),
        check_vma=False,
    )
```

time: 903 us -> 142 us (0.16)
  waiting for transfers between devices: 552 us -> 0 us
  local copies, waits for them, and re-layouts: 236 us -> 5.62 us
  Pallas kernels: 0 us -> 131 us
  matrix products: 48.5 us -> 0 us
  starting transfers between devices: 27.8 us -> 0 us
  other arithmetic: 21.2 us -> 4.89 us
  between operations: 13.5 us -> 0.03 us
    all_to_all x2 -> x0, waiting for transfers between devices: 505 us -> none  [the longest x1 494 us: body(): lax.all_to_all(kv_sent, 'gz', split_axis=0, concat_axis=0, tiled=True)]
    pallas_call x0 -> x2, Pallas kernels: none -> 131 us  [the longest x1 96.2 us: exchange(): pl.pallas_call(comm_kernel, name='exchange', out_shape=(jax.ShapeDtypeStr...]
    gather x17 -> x0, local copies, waits for them, and re-layouts: 69.7 us -> none  [the longest x16 61.5 us: one_block(): gathered = jnp.concatenate([slab_kv[near_row], far_kv[slot_row]], axis=0)]
    slice x29 -> x2, local copies, waits for them, and re-layouts: 69.4 us -> 2.22 us  [the longest x1 2.15 us: body(): qkv_weight[:, 2 * width:]]
    dot_general x19 -> x0, matrix products: 48.5 us -> none  [the longest x8 25.1 us: attend(): jnp.einsum('hqk,khd->qhd', weights.astype(jnp.bfloat16), values, preferre...]
    all_gather x1 -> x0, waiting for transfers between devices: 46.9 us -> none  [body(): slab_kv = lax.all_gather(kv_own, 'row', axis=0, tiled=True)]
    reshape x16 -> x3, local copies, waits for them, and re-layouts: 37.9 us -> 2.56 us  [the longest x1 1.25 us: body(): norm_gain.reshape(1, 1, width)]
    all_to_all x2 -> x0, starting transfers between devices: 27.6 us -> none  [the longest x1 20.6 us: body(): lax.all_to_all(request.reshape(slabs_n, per_owner), 'gz', split_axis=0, c...]
  transfers between devices with their start and end apart: 3 -> 0, of which waited for: 3 -> 0; matrix products, arithmetic and copies ran while one was open for 1% -> 0% of each run, Pallas kernels for 0% -> 0%
where the time goes in v1:
time: 142 us; the launch traced here: 141 us
  Pallas kernels  131 us (92%)
  local copies, waits for them, and re-layouts  5.62 us (4%)
  other arithmetic  4.89 us (3%)
    pallas_call x1, Pallas kernels, exchange(): pl.pallas_call(comm_kernel, name='exchange', out_shape=(jax.ShapeDtypeStr...  96.2 us
    pallas_call x1, Pallas kernels, attention(): pl.pallas_call(block_kernel, name='attention', out_shape=jax.ShapeDtypeSt...  34.7 us

profile of v1, /device:TPU:1, one launch (start us, length us, event | category | flops | bytes accessed | tf_op | source)
XLA Modules:
  0.0 141.4 jit_solution(7294675855728149640)
XLA Ops:
  0.0 1.3 reshape.142.gain_ref
  1.3 1.2 reshape.148.gain_ref
  2.5 0.1 broadcast_add_fusion
  2.6 0.8 add_select_fusion
  3.4 0.1 reshape.143
  3.4 1.3 add_select_fusion.5
  4.8 0.1 slice.15
  4.8 0.1 eq.74
  4.9 0.3 select_reduce_fusion.1
  5.2 0.6 pad.4
  5.8 0.1 copy.10
  5.9 1.1 select_reduce_fusion
  7.0 0.1 copy.11
  7.1 1.3 compare_convert_fusion.live_ref
  8.4 2.1 %fusion.24 = (bf16[384,384]{1,0:T(8,128)(2,1)}, bf16[384,384]{1,0:T(8,128)(2,1)}, bf16[384,384]{1,0:T(8,128)(2,1)}) fusion(bf16[384,1152]{1,0:T(8,128)(2,1)} %param.13), kind=kLoop, calls=%fused_computation.81 | loop fusion | bytes 1769472 | tf_op jit(solution)/shard_map/slice | solution.py:315
  10.5 96.2 %exchange.1 = (bf16[8,16,64,384]{3,2,1,0:T(8,128)(2,1)}, bf16[4,8,64,384]{3,2,1,0:T(8,128)(2,1)}, bf16[8,64,384]{2,1,0:T(8,128)(2,1)}) custom-call(bf16[8,64,384]{2,1,0:T(8,128)(2,1)} %bitcast.6, f32[1,1,384]{2,1,0:T(1,128)} %reshape.142.gain_ref, s32[8,1,128]{2,1,0:T(1,128)} %bitcast.9), custom_call_target="tpu_custom_call" | custom-call | tf_op jit(solution)/shard_map/exchange/pallas_call | solution.py:160
  106.7 34.7 %attention.1 = bf16[512,384]{1,0:T(8,128)(2,1)} custom-call(s32[8,20]{1,0:T(8,128)} %get-tuple-element.15.pos_ref, s32[8,20]{1,0:T(8,128)} %compare_convert_fusion.live_ref, bf16[512,384]{1,0:T(8,128)(2,1)} %tok_ref.1, bf16[512,384]{1,0:T(8,128)(2,1)} %bitcast.8, bf16[128,64,384]{2,1,0:T(8,128)(2,1)} %bitcast.5, bf16[32,64,384]{2,1,0:T(8,128)(2,1)} %bitcast.7, ...), custom_call_target="tpu_custom_call" | custom-call | tf_op jit(solution)/shard_map/attention/pallas_call | solution.py:262
  (3 shorter events, 0.0 us)

commit v2 on v0

v2 whole, which is shorter than its diff:
```python
import functools

import jax
import jax.numpy as jnp
from jax import lax
from jax.experimental import pallas as pl
from jax.experimental.pallas import tpu as pltpu
from jax.sharding import PartitionSpec as P

H = 12
NNEAR = 4
NFAR = 16
NZ = 16
NJ = 8
NX = 4
BLOCK = 64
HEADS = 6
LANES = 256
SPARE = 192
ROWS = (48, 16)
PIECES = 4
MESH = pl.DeviceIdType.MESH
F32, BF16 = jnp.float32, jnp.bfloat16


def rms_norm(values, gain):
    mean_sq = jnp.mean(values * values, axis=-1, keepdims=True)
    return values * lax.rsqrt(mean_sq + 1e-05) * gain


def matmul(a, b):
    return jnp.dot(a, b, preferred_element_type=F32)


def ring_places(k):
    return (0, 1) if k == 0 else (15, 1) if k == 8 else (2 * k - 1, 2)


def fused_kernel(
    kb_ref, counts_ref, tok_ref, gain_ref, gain2_ref, qkv_any, wo_any, up_any, down_any, out_ref, *scratch
):
    scratch = list(scratch)
    passes = len(ROWS)

    def take(n):
        got = scratch[:n]
        del scratch[:n]
        return got

    own_rows = take(passes)
    slots = [take(15) for _ in range(passes)]
    send = take(passes)
    far = take(passes)
    kv_far = take(passes)
    kv_near = take(passes)
    near, normed, qkv_w, wo_w, up_w, down_w = take(6)
    wq_x, wkv_x, wo_x, q_ref, stage, s_ref, p_ref, acc_ref, top_ref, att = take(10)
    req_out, req_in, req_s = take(3)
    fs_sem, fr_sem, bs_sem, br_sem, ys_sem, yr_sem, xs_sem, xr_sem, qs_sem, qr_sem, loc_sem = take(11)

    tokens, width = tok_ref.shape
    own = tokens // BLOCK
    gz = lax.axis_index("gz")
    x = lax.axis_index("row")
    z = gz // NJ
    j = lax.rem(gz, NJ)
    z_up = lax.rem(z + 1, NZ) * NJ + j
    z_down = lax.rem(z + NZ - 1, NZ) * NJ + j

    def plane(o):
        return z * NJ + lax.rem(j + o, NJ)

    def along(o):
        return lax.rem(x + o, NX)

    barrier = pltpu.get_barrier_semaphore()
    for peer in (z_up, z_down):
        pl.semaphore_signal(barrier, inc=1, device_id=(peer, x), device_id_type=MESH)
    for o in range(1, NJ):
        pl.semaphore_signal(barrier, inc=1, device_id=(plane(o), x), device_id_type=MESH)
    for o in range(1, NX):
        pl.semaphore_signal(barrier, inc=1, device_id=(gz, along(o)), device_id_type=MESH)

    weights = [
        pltpu.make_async_copy(src, dst, loc_sem.at[i])
        for i, (src, dst) in enumerate(
            ((qkv_any, qkv_w), (wo_any, wo_w), (up_any, up_w), (down_any, down_w)))
    ]
    for copy in weights:
        copy.start()

    normed[...] = rms_norm(tok_ref[...].astype(F32), gain_ref[...]).astype(BF16)
    first = 0
    for m, rows in enumerate(ROWS):
        for b in range(own):
            own_rows[m][b] = normed[b * BLOCK + first:b * BLOCK + first + rows]
        first += rows
    for b in range(own):
        near[0, b] = normed[b * BLOCK:(b + 1) * BLOCK]

    place = lax.broadcasted_iota(jnp.int32, (NJ, 128), 1)
    offset = lax.broadcasted_iota(jnp.int32, (NJ, 128), 0)
    z_off = jnp.where(place == 15, 8, jnp.where((place & 1) == 1, (place + 1) >> 1, NZ - (place >> 1)))
    slab = ((z + z_off) & (NZ - 1)) * NJ + ((j + offset) & (NJ - 1))
    wanted = jnp.zeros((NJ, 128), jnp.int32)
    for b in range(own):
        for n in range(NNEAR, NNEAR + NFAR):
            block = kb_ref[b, n]
            wanted = jnp.where(slab == (block >> 5), block & 7, wanted)
    for r in range(NJ):
        req_out[r] = wanted[r:r + 1]
    req_in[0] = wanted[0:1]

    pl.semaphore_wait(barrier, 2 + NJ - 1 + NX - 1)

    def req_copy(o):
        return pltpu.make_async_remote_copy(
            src_ref=req_out.at[NJ - o], dst_ref=req_in.at[o],
            send_sem=qs_sem.at[o], recv_sem=qr_sem.at[o],
            device_id=(plane(NJ - o), x), device_id_type=MESH)

    def ring(m, k, h, up):
        src = own_rows[m] if k == 1 else slots[m][(0 if up else 7) + k - 2]
        dst = slots[m][14] if k == 8 else slots[m][(0 if up else 7) + k - 1]
        size = NJ // PIECES
        part = pl.ds(h * size, size)
        return pltpu.make_async_remote_copy(
            src_ref=src.at[part], dst_ref=dst.at[part],
            send_sem=(fs_sem if up else bs_sem).at[m, k, h],
            recv_sem=(fr_sem if up else br_sem).at[m, k, h],
            device_id=(z_up if up else z_down, x), device_id_type=MESH)

    def in_ring(k, h, up):
        return k < 8 or (k == 8 and (h < PIECES // 2) == up)

    def near_copy(o):
        return pltpu.make_async_remote_copy(
            src_ref=near.at[0], dst_ref=near.at[o],
            send_sem=xs_sem.at[o], recv_sem=xr_sem.at[o],
            device_id=(gz, along(o)), device_id_type=MESH)

    def plane_copy(m, k, o, count):
        at = pl.ds(*ring_places(k))
        to = pl.ds(o, count)
        return pltpu.make_async_remote_copy(
            src_ref=send[m].at[to, at], dst_ref=far[m].at[to, at],
            send_sem=ys_sem.at[m, k], recv_sem=yr_sem.at[m, k],
            device_id=(plane(o), x), device_id_type=MESH)

    def to_plane(m, k):
        at, count = ring_places(k)
        if k == 0:
            held = [(0, own_rows[m])]
        elif k == 8:
            held = [(15, slots[m][14])]
        else:
            held = [(at, slots[m][7 + k - 1]), (at + 1, slots[m][k - 1])]

        def one(o, carry):
            for p, ref in held:
                send[m][o, p] = ref[req_s[o, 0, p]]
            plane_copy(m, k, o, 1).start()
            return carry

        lax.fori_loop(1, NJ, one, 0)
        for p, ref in held:
            far[m][0, p] = ref[req_s[0, 0, p]]

    lane = lax.broadcasted_iota(jnp.int32, (1, LANES), 1)

    def prepare():
        row = lax.broadcasted_iota(jnp.int32, (width, 2 * LANES), 0)
        col = lax.broadcasted_iota(jnp.int32, (width, 2 * LANES), 1)
        inner = col & (LANES - 1)
        spread = ((inner < SPARE) & (row == (col >> 8) * SPARE + inner)).astype(F32).astype(BF16)
        weights[0].wait()
        wq_x[...] = matmul(qkv_w[:, :width], spread).astype(BF16)
        for i in range(2):
            wkv_x[:, i * 2 * LANES:(i + 1) * 2 * LANES] = matmul(
                qkv_w[:, (1 + i) * width:(2 + i) * width], spread).astype(BF16)
        weights[1].wait()
        wo_x[...] = lax.dot_general(
            spread, wo_w[...], (((0,), (0,)), ((), ())), preferred_element_type=F32).astype(BF16)

    def fold_queries():
        scale = 1.4426950408889634 / ((width // H) ** 0.5)
        queries = (matmul(normed[...], wq_x[...]) * scale).astype(BF16)
        lanes = lax.broadcasted_iota(jnp.int32, (tokens, LANES), 1)
        for g in range(2):
            part = queries[:, g * LANES:(g + 1) * LANES]
            for i in range(HEADS):
                one = jnp.where(
                    lanes // 32 == i, part, jnp.where(lanes == SPARE, 1.0, 0.0).astype(BF16))
                for b in range(own):
                    q_ref[b, g, i * BLOCK:(i + 1) * BLOCK] = one[b * BLOCK:(b + 1) * BLOCK]

    def project(values):
        lanes = lax.broadcasted_iota(jnp.int32, (1, 4 * LANES), 1)
        inner = lanes & (LANES - 1)
        ones = jnp.where((lanes >= 2 * LANES) & (inner >= SPARE) & (inner < SPARE + HEADS), 1.0, 0.0)
        return (matmul(values, wkv_x[...]) + ones).astype(BF16)

    def project_far(m, k):
        rows = ROWS[m]
        at, count = ring_places(k)
        plane_copy(m, k, 1, NJ - 1).wait_recv()
        for o in range(0, NJ, 4):
            got = project(far[m][o:o + 4, at:at + count].reshape(4 * count * rows, width))
            kv_far[m][o:o + 4, at:at + count] = got.reshape(4, count, rows, 4 * LANES)

    def project_near(o):
        if o:
            near_copy(o).wait_recv()
        got = project(near[o].reshape(own * BLOCK, width))
        first = 0
        for m, rows in enumerate(ROWS):
            for b in range(own):
                kv_near[m][o, b] = got[b * BLOCK + first:b * BLOCK + first + rows]
            first += rows

    def attend(m, b):
        rows = ROWS[m]
        keys = (NNEAR + NFAR) * rows
        lanes = lax.broadcasted_iota(jnp.int32, (rows, 2 * LANES), 1)
        is_bias = (lanes & (LANES - 1)) == SPARE
        for n in range(NNEAR + NFAR):
            block = kb_ref[b, n]
            owner = block >> 5
            within = block & 31
            bias = jnp.where(within < counts_ref[owner], 0.0, -1e30)
            if n < NNEAR:
                got = kv_near[m][(x - (within >> 3)) & (NX - 1), within & 7]
            else:
                z_rel = ((owner >> 3) - z) & (NZ - 1)
                at = jnp.where(z_rel == 0, 0, jnp.where(
                    z_rel == 8, 15, jnp.where(z_rel < 8, 2 * z_rel - 1, 2 * (NZ - z_rel))))
                got = kv_far[m][(j - (owner & 7)) & (NJ - 1), at]
            part = slice(n * rows, (n + 1) * rows)
            stage[part, :2 * LANES] = jnp.where(is_bias, bias.astype(BF16), got[:, :2 * LANES])
            stage[part, 2 * LANES:] = got[:, 2 * LANES:]
        lane_b = lax.broadcasted_iota(jnp.int32, (BLOCK, LANES), 1)
        lane_t = lax.broadcasted_iota(jnp.int32, (BLOCK, 128), 1)
        for g in range(2):
            s_ref[:, :keys] = lax.dot_general(
                q_ref[b, g], stage[:keys, g * LANES:(g + 1) * LANES], (((1,), (1,)), ((), ())),
                preferred_element_type=F32)
            tops, alphas = [], []
            for i in range(HEADS):
                part = slice(i * BLOCK, (i + 1) * BLOCK)
                scores = s_ref[part, :keys]
                top = jnp.max(scores, axis=-1, keepdims=True)
                if m > 0:
                    before = top_ref[b, g, :, i:i + 1]
                    top = jnp.maximum(top, before)
                    alphas.append(jnp.exp2(before - top))
                tops.append(top)
                p_ref[part, :keys] = jnp.exp2(scores - top).astype(BF16)
            mixed = matmul(p_ref[:, :keys], stage[:keys, (2 + g) * LANES:(3 + g) * LANES])
            total = jnp.zeros((BLOCK, LANES), F32)
            kept = jnp.zeros((BLOCK, LANES), F32)
            for i in range(HEADS):
                mine = (lane_b // 32 == i) | (lane_b == SPARE + i)
                total = jnp.where(mine, mixed[i * BLOCK:(i + 1) * BLOCK], total)
                if m > 0:
                    kept = jnp.where(mine, alphas[i], kept)
            if m > 0:
                total = total + kept * acc_ref[b, g]
            if m < passes - 1:
                acc_ref[b, g] = total
                highest = jnp.zeros((BLOCK, 128), F32)
                for i in range(HEADS):
                    highest = jnp.where(lane_t == i, tops[i], highest)
                top_ref[b, g] = highest
            else:
                denom = jnp.ones((BLOCK, LANES), F32)
                for i in range(HEADS):
                    denom = jnp.where(lane_b // 32 == i, total[:, SPARE + i:SPARE + i + 1], denom)
                result = jnp.where(lane_b < SPARE, total / denom, 0.0)
                att[pl.ds(b * BLOCK, BLOCK), g * LANES:(g + 1) * LANES] = result.astype(BF16)

    def start_ring(m):
        for h in range(PIECES):
            ring(m, 1, h, True).start()
            ring(m, 1, h, False).start()

    for o in range(1, NJ):
        req_copy(o).start()
    start_ring(0)
    for o in range(1, NX):
        near_copy(o).start()
    for o in range(1, NJ):
        req_copy(o).wait_recv()
    copy = pltpu.make_async_copy(req_in, req_s, loc_sem.at[4])
    copy.start()
    copy.wait()

    ticks = [(m, k) for m in range(passes) for k in range(9)]
    work = {}

    def put(tick, task):
        work.setdefault(tick, []).append(task)

    put(0, prepare)
    put(0, fold_queries)
    for o in range(NX):
        put(1 + o, functools.partial(project_near, o))
    for t, (m, k) in enumerate(ticks):
        put(t + 2, functools.partial(project_far, m, k))
    for m in range(passes - 1):
        for b in range(own):
            put(9 * m + 10 + b, functools.partial(attend, m, b))

    for t, (m, k) in enumerate(ticks):
        if k > 0:
            for h in range(PIECES):
                for up in (True, False):
                    if in_ring(k, h, up):
                        ring(m, k, h, up).wait_recv()
                        if in_ring(k + 1, h, up):
                            ring(m, k + 1, h, up).start()
            if k == 7 and m + 1 < passes:
                start_ring(m + 1)
        to_plane(m, k)
        for task in work.pop(t, []):
            task()
    for t in sorted(work):
        for task in work[t]:
            task()

    def last(b, carry):
        attend(passes - 1, b)
        return carry

    lax.fori_loop(0, own, last, 0)

    residual = (tok_ref[...].astype(F32) + matmul(att[...], wo_x[...])).astype(BF16).astype(F32)
    second = rms_norm(residual, gain2_ref[...]).astype(BF16)
    weights[2].wait()
    hidden = jax.nn.gelu(matmul(second, up_w[...])).astype(BF16)
    weights[3].wait()
    out_ref[...] = (residual + matmul(hidden, down_w[...])).astype(BF16)

    for m, k in ticks:
        for h in range(PIECES):
            for up in (True, False):
                if k > 0 and in_ring(k, h, up):
                    ring(m, k, h, up).wait_send()
        plane_copy(m, k, 1, NJ - 1).wait_send()
    for o in range(1, NX):
        near_copy(o).wait_send()
    for o in range(1, NJ):
        req_copy(o).wait_send()


def body(
    tokens, key_blocks, counts, norm_gain, qkv_weight, out_weight, mlp_gain, up_weight, down_weight
):
    count, width = tokens.shape
    own = key_blocks.shape[0]
    passes = len(ROWS)
    vmem = pl.BlockSpec(memory_space=pltpu.VMEM)
    smem = pl.BlockSpec(memory_space=pltpu.SMEM)
    anywhere = pl.BlockSpec(memory_space=pl.ANY)
    dma = pltpu.SemaphoreType.DMA

    def buffers(*shape):
        return [pltpu.VMEM(tuple(rows if n == "rows" else n for n in shape), BF16) for rows in ROWS]

    slots = [pltpu.VMEM((own, rows, width), BF16) for rows in ROWS for _ in range(15)]
    keys = (NNEAR + NFAR) * max(ROWS)
    return pl.pallas_call(
        fused_kernel,
        name="block",
        out_shape=jax.ShapeDtypeStruct(tokens.shape, BF16),
        in_specs=[smem] * 2 + [vmem] * 3 + [anywhere] * 4,
        out_specs=vmem,
        scratch_shapes=buffers(own, "rows", width)
        + slots
        + buffers(NJ, NZ, "rows", width)
        + buffers(NJ, NZ, "rows", width)
        + buffers(NJ, NZ, "rows", 4 * LANES)
        + buffers(NX, own, "rows", 4 * LANES)
        + [
            pltpu.VMEM((NX, own, BLOCK, width), BF16),
            pltpu.VMEM((count, width), BF16),
            pltpu.VMEM(qkv_weight.shape, BF16),
            pltpu.VMEM(out_weight.shape, BF16),
            pltpu.VMEM(up_weight.shape, BF16),
            pltpu.VMEM(down_weight.shape, BF16),
            pltpu.VMEM((width, 2 * LANES), BF16),
            pltpu.VMEM((width, 4 * LANES), BF16),
            pltpu.VMEM((2 * LANES, width), BF16),
            pltpu.VMEM((own, 2, HEADS * BLOCK, LANES), BF16),
            pltpu.VMEM((keys, 4 * LANES), BF16),
            pltpu.VMEM((HEADS * BLOCK, keys), F32),
            pltpu.VMEM((HEADS * BLOCK, keys), BF16),
            pltpu.VMEM((own, 2, BLOCK, LANES), F32),
            pltpu.VMEM((own, 2, BLOCK, 128), F32),
            pltpu.VMEM((count, 2 * LANES), BF16),
            pltpu.VMEM((NJ, 1, 128), jnp.int32),
            pltpu.VMEM((NJ, 1, 128), jnp.int32),
            pltpu.SMEM((NJ, 1, 128), jnp.int32),
            dma((passes, 9, PIECES)), dma((passes, 9, PIECES)), dma((passes, 9, PIECES)), dma((passes, 9, PIECES)),
            dma((passes, 9)), dma((passes, 9)),
            dma((NX,)), dma((NX,)),
            dma((NJ,)), dma((NJ,)),
            dma((5,)),
        ],
        compiler_params=pltpu.CompilerParams(
            collective_id=0, has_side_effects=True, vmem_limit_bytes=62 << 20
        ),
    )(key_blocks, counts, tokens, norm_gain, mlp_gain, qkv_weight, out_weight, up_weight, down_weight)


def solution(mesh):
    return jax.shard_map(
        body,
        mesh=mesh,
        in_specs=(
            P(("gz", "row"), None),
            P(("gz", "row"), None),
            P(),
            P(),
            P(),
            P(),
            P(),
            P(),
            P(),
        ),
        out_specs=P(("gz", "row"), None),
        check_vma=False,
    )
```

time: 903 us -> 125 us (0.14)
  waiting for transfers between devices: 552 us -> 0 us
  local copies, waits for them, and re-layouts: 236 us -> 1.78 us
  Pallas kernels: 0 us -> 123 us
  matrix products: 48.5 us -> 0 us
  starting transfers between devices: 27.8 us -> 0 us
  other arithmetic: 21.2 us -> 0 us
  between operations: 13.5 us -> 0.01 us
    all_to_all x2 -> x0, waiting for transfers between devices: 505 us -> none  [the longest x1 494 us: body(): lax.all_to_all(kv_sent, 'gz', split_axis=0, concat_axis=0, tiled=True)]
    pallas_call x0 -> x1, Pallas kernels: none -> 123 us  [body(): pl.pallas_call(fused_kernel, name='block', out_shape=jax.ShapeDtypeStruct...]
    gather x17 -> x0, local copies, waits for them, and re-layouts: 69.7 us -> none  [the longest x16 61.5 us: one_block(): gathered = jnp.concatenate([slab_kv[near_row], far_kv[slot_row]], axis=0)]
    slice x29 -> x0, local copies, waits for them, and re-layouts: 69.4 us -> none  [the longest x16 46.1 us: attend(): keys = key_values[:, :, :model_width].reshape(-1, H, head_size)]
    dot_general x19 -> x0, matrix products: 48.5 us -> none  [the longest x8 25.1 us: attend(): jnp.einsum('hqk,khd->qhd', weights.astype(jnp.bfloat16), values, preferre...]
    all_gather x1 -> x0, waiting for transfers between devices: 46.9 us -> none  [body(): slab_kv = lax.all_gather(kv_own, 'row', axis=0, tiled=True)]
    reshape x16 -> x0, local copies, waits for them, and re-layouts: 37.9 us -> none  [the longest x8 19 us: attend(): keys = key_values[:, :, :model_width].reshape(-1, H, head_size)]
    all_to_all x2 -> x0, starting transfers between devices: 27.6 us -> none  [the longest x1 20.6 us: body(): lax.all_to_all(request.reshape(slabs_n, per_owner), 'gz', split_axis=0, c...]
  transfers between devices with their start and end apart: 3 -> 0, of which waited for: 3 -> 0; matrix products, arithmetic and copies ran while one was open for 1% -> 0% of each run, Pallas kernels for 0% -> 0%
where the time goes in v2:
time: 125 us
  Pallas kernels  123 us (98%)
  local copies, waits for them, and re-layouts  1.78 us (1%)
    pallas_call x1, Pallas kernels, body(): pl.pallas_call(fused_kernel, name='block', out_shape=jax.ShapeDtypeStruct...  123 us

profile of v2, /device:TPU:1, one launch (start us, length us, event | category | flops | bytes accessed | tf_op | source)
XLA Modules:
  0.0 125.0 jit_solution(13896403685105739148)
XLA Ops:
  0.0 123.2 %block.1 = bf16[512,384]{1,0:T(8,128)(2,1)} custom-call(s32[8,20]{1,0:T(8,128)} %kb_ref.1, s32[128]{0:T(128)} %counts_ref.1, bf16[512,384]{1,0:T(8,128)(2,1)} %tok_ref.1, f32[384]{0:T(512)} %gain_ref.1, f32[384]{0:T(512)} %gain2_ref.1, bf16[384,1152]{1,0:T(8,128)(2,1)} %qkv_any.1, bf16[384,384]{1,0:T(8,128)(2,1)} %wo_any.1, bf16[384,1536]{1,0:T(8,128)(2,1)} %up_any.1, ...), custom_call_target="tpu_custom_call" | custom-call | tf_op jit(solution)/shard_map/block/pallas_call | solution.py:371
  123.2 1.8 %copy.11 = bf16[512,384]{1,0:T(8,128)(2,1)} copy(bf16[512,384]{1,0:T(8,128)(2,1)} %block.1) | data formatting | bytes 786432

commit v3 on v2

--- a/solution.py
+++ b/solution.py
@@ -17,8 +17,9 @@
 HEADS = 6
 LANES = 256
 SPARE = 192
-ROWS = (48, 16)
-PIECES = 4
+ROWS = (32, 32)
+LAG = 2
+PIECES = 2
 MESH = pl.DeviceIdType.MESH
 F32, BF16 = jnp.float32, jnp.bfloat16
 
@@ -54,7 +55,8 @@
     kv_far = take(passes)
     kv_near = take(passes)
     near, normed, qkv_w, wo_w, up_w, down_w = take(6)
-    wq_x, wkv_x, wo_x, q_ref, stage, s_ref, p_ref, acc_ref, top_ref, att = take(10)
+    wq_x, wkv_x, wo_x, q_ref, acc_ref, top_ref, att = take(7)
+    stages, s_refs, p_refs = take(2), take(4), take(4)
     req_out, req_in, req_s = take(3)
     fs_sem, fr_sem, bs_sem, br_sem, ys_sem, yr_sem, xs_sem, xr_sem, qs_sem, qr_sem, loc_sem = take(11)
 
@@ -95,23 +97,21 @@
         for b in range(own):
             own_rows[m][b] = normed[b * BLOCK + first:b * BLOCK + first + rows]
         first += rows
-    for b in range(own):
-        near[0, b] = normed[b * BLOCK:(b + 1) * BLOCK]
-
-    place = lax.broadcasted_iota(jnp.int32, (NJ, 128), 1)
-    offset = lax.broadcasted_iota(jnp.int32, (NJ, 128), 0)
-    z_off = jnp.where(place == 15, 8, jnp.where((place & 1) == 1, (place + 1) >> 1, NZ - (place >> 1)))
-    slab = ((z + z_off) & (NZ - 1)) * NJ + ((j + offset) & (NJ - 1))
-    wanted = jnp.zeros((NJ, 128), jnp.int32)
-    for b in range(own):
-        for n in range(NNEAR, NNEAR + NFAR):
-            block = kb_ref[b, n]
-            wanted = jnp.where(slab == (block >> 5), block & 7, wanted)
-    for r in range(NJ):
-        req_out[r] = wanted[r:r + 1]
-    req_in[0] = wanted[0:1]
-
     pl.semaphore_wait(barrier, 2 + NJ - 1 + NX - 1)
+
+    def make_requests():
+        place = lax.broadcasted_iota(jnp.int32, (NJ, 128), 1)
+        offset = lax.broadcasted_iota(jnp.int32, (NJ, 128), 0)
+        z_off = jnp.where(place == 15, 8, jnp.where((place & 1) == 1, (place + 1) >> 1, NZ - (place >> 1)))
+        slab = ((z + z_off) & (NZ - 1)) * NJ + ((j + offset) & (NJ - 1))
+        wanted = jnp.zeros((NJ, 128), jnp.int32)
+        for b in range(own):
+            for n in range(NNEAR, NNEAR + NFAR):
+                block = kb_ref[b, n]
+                wanted = jnp.where(slab == (block >> 5), block & 7, wanted)
+        for r in range(NJ):
+            req_out[r] = wanted[r:r + 1]
+        req_in[0] = wanted[0:1]
 
     def req_copy(o):
         return pltpu.make_async_remote_copy(
@@ -218,9 +218,13 @@
                 kv_near[m][o, b] = got[b * BLOCK + first:b * BLOCK + first + rows]
             first += rows
 
-    def attend(m, b):
+    lane_b = lax.broadcasted_iota(jnp.int32, (1, LANES), 1)
+    lane_t = lax.broadcasted_iota(jnp.int32, (1, 128), 1)
+    head_lanes = [(lane_b >> 5) == i for i in range(HEADS)]
+    mine = [head_lanes[i] | (lane_b == SPARE + i) for i in range(HEADS)]
+
+    def fill(m, b, stage):
         rows = ROWS[m]
-        keys = (NNEAR + NFAR) * rows
         lanes = lax.broadcasted_iota(jnp.int32, (rows, 2 * LANES), 1)
         is_bias = (lanes & (LANES - 1)) == SPARE
         for n in range(NNEAR + NFAR):
@@ -238,54 +242,74 @@
             part = slice(n * rows, (n + 1) * rows)
             stage[part, :2 * LANES] = jnp.where(is_bias, bias.astype(BF16), got[:, :2 * LANES])
             stage[part, 2 * LANES:] = got[:, 2 * LANES:]
-        lane_b = lax.broadcasted_iota(jnp.int32, (BLOCK, LANES), 1)
-        lane_t = lax.broadcasted_iota(jnp.int32, (BLOCK, 128), 1)
+
+    def softmax(m, s_ref, p_ref):
+        keys = (NNEAR + NFAR) * ROWS[m]
+        tops = []
+        for i in range(HEADS):
+            part = slice(i * BLOCK, (i + 1) * BLOCK)
+            scores = s_ref[part, :keys]
+            top = jnp.max(scores, axis=-1, keepdims=True)
+            tops.append(top)
+            p_ref[part, :keys] = jnp.exp2(scores - top).astype(BF16)
+        return tops
+
+    def keep(m, b, g, mixed, tops):
+        total = jnp.zeros((BLOCK, LANES), F32)
+        highest = jnp.zeros((BLOCK, 128), F32)
+        for i in range(HEADS):
+            total = jnp.where(mine[i], mixed[i * BLOCK:(i + 1) * BLOCK], total)
+            highest = jnp.where(lane_t == i, tops[i], highest)
+        rows = pl.ds(b * BLOCK, BLOCK)
+        acc_ref[m, g, rows] = total
+        top_ref[m, g, rows] = highest
+
+    def select(values, chosen):
+        high = values.astype(BF16)
+        low = (values - high.astype(F32)).astype(BF16)
+        return matmul(high, chosen) + matmul(low, chosen)
+
+    def join():
+        row = lax.broadcasted_iota(jnp.int32, (128, LANES), 0)
+        col = lax.broadcasted_iota(jnp.int32, (128, LANES), 1)
+        spread = ((row < HEADS) & ((row == (col >> 5)) | (col == SPARE + row))).astype(F32).astype(BF16)
+        row = lax.broadcasted_iota(jnp.int32, (LANES, LANES), 0)
+        col = lax.broadcasted_iota(jnp.int32, (LANES, LANES), 1)
+        source = jnp.where(col < SPARE, SPARE + (col >> 5), SPARE)
+        totals = (row == source).astype(F32).astype(BF16)
         for g in range(2):
-            s_ref[:, :keys] = lax.dot_general(
-                q_ref[b, g], stage[:keys, g * LANES:(g + 1) * LANES], (((1,), (1,)), ((), ())),
+            tops = [top_ref[m, g] for m in range(passes)]
+            highest = functools.reduce(jnp.maximum, tops)
+            total = sum(
+                select(jnp.exp2(tops[m] - highest), spread) * acc_ref[m, g] for m in range(passes))
+            result = jnp.where(lane_b < SPARE, total / select(total, totals), 0.0)
+            att[:, g * LANES:(g + 1) * LANES] = result.astype(BF16)
+
+    def attend(m, first):
+        keys = (NNEAR + NFAR) * ROWS[m]
+        chains = [(c, first + c // 2, c % 2) for c in range(4)]
+        for c in range(2):
+            fill(m, first + c, stages[c])
+        for c, b, g in chains:
+            s_refs[c][:, :keys] = lax.dot_general(
+                q_ref[b, g], stages[c // 2][:keys, g * LANES:(g + 1) * LANES], (((1,), (1,)), ((), ())),
                 preferred_element_type=F32)
-            tops, alphas = [], []
-            for i in range(HEADS):
-                part = slice(i * BLOCK, (i + 1) * BLOCK)
-                scores = s_ref[part, :keys]
-                top = jnp.max(scores, axis=-1, keepdims=True)
-                if m > 0:
-                    before = top_ref[b, g, :, i:i + 1]
-                    top = jnp.maximum(top, before)
-                    alphas.append(jnp.exp2(before - top))
-                tops.append(top)
-                p_ref[part, :keys] = jnp.exp2(scores - top).astype(BF16)
-            mixed = matmul(p_ref[:, :keys], stage[:keys, (2 + g) * LANES:(3 + g) * LANES])
-            total = jnp.zeros((BLOCK, LANES), F32)
-            kept = jnp.zeros((BLOCK, LANES), F32)
-            for i in range(HEADS):
-                mine = (lane_b // 32 == i) | (lane_b == SPARE + i)
-                total = jnp.where(mine, mixed[i * BLOCK:(i + 1) * BLOCK], total)
-                if m > 0:
-                    kept = jnp.where(mine, alphas[i], kept)
-            if m > 0:
-                total = total + kept * acc_ref[b, g]
-            if m < passes - 1:
-                acc_ref[b, g] = total
-                highest = jnp.zeros((BLOCK, 128), F32)
-                for i in range(HEADS):
-                    highest = jnp.where(lane_t == i, tops[i], highest)
-                top_ref[b, g] = highest
-            else:
-                denom = jnp.ones((BLOCK, LANES), F32)
-                for i in range(HEADS):
-                    denom = jnp.where(lane_b // 32 == i, total[:, SPARE + i:SPARE + i + 1], denom)
-                result = jnp.where(lane_b < SPARE, total / denom, 0.0)
-                att[pl.ds(b * BLOCK, BLOCK), g * LANES:(g + 1) * LANES] = result.astype(BF16)
+        found = [softmax(m, s_refs[c], p_refs[c]) for c, b, g in chains]
+        for c, b, g in chains:
+            mixed = matmul(p_refs[c][:, :keys], stages[c // 2][:keys, (2 + g) * LANES:(3 + g) * LANES])
+            keep(m, b, g, mixed, found[c])
 
     def start_ring(m):
         for h in range(PIECES):
             ring(m, 1, h, True).start()
             ring(m, 1, h, False).start()
 
+    start_ring(0)
+    make_requests()
     for o in range(1, NJ):
         req_copy(o).start()
-    start_ring(0)
+    for b in range(own):
+        near[0, b] = normed[b * BLOCK:(b + 1) * BLOCK]
     for o in range(1, NX):
         near_copy(o).start()
     for o in range(1, NJ):
@@ -294,7 +318,7 @@
     copy.start()
     copy.wait()
 
-    ticks = [(m, k) for m in range(passes) for k in range(9)]
+    ticks = 9 + LAG * (passes - 1)
     work = {}
 
     def put(tick, task):
@@ -304,34 +328,41 @@
     put(0, fold_queries)
     for o in range(NX):
         put(1 + o, functools.partial(project_near, o))
-    for t, (m, k) in enumerate(ticks):
-        put(t + 2, functools.partial(project_far, m, k))
+    for t in range(ticks):
+        for m in range(passes):
+            if 0 <= t - m * LAG <= 8:
+                put(t + 1, functools.partial(project_far, m, t - m * LAG))
     for m in range(passes - 1):
-        for b in range(own):
-            put(9 * m + 10 + b, functools.partial(attend, m, b))
-
-    for t, (m, k) in enumerate(ticks):
-        if k > 0:
+        for i in range(own // 2):
+            put(min(9 + m * LAG + i, ticks - 1), functools.partial(attend, m, 2 * i))
+
+    for t in range(ticks):
+        active = [(m, t - m * LAG) for m in range(passes) if 0 <= t - m * LAG <= 8]
+        for m, k in active:
+            if k == 0:
+                if m:
+                    start_ring(m)
+                continue
             for h in range(PIECES):
                 for up in (True, False):
                     if in_ring(k, h, up):
                         ring(m, k, h, up).wait_recv()
                         if in_ring(k + 1, h, up):
                             ring(m, k + 1, h, up).start()
-            if k == 7 and m + 1 < passes:
-                start_ring(m + 1)
-        to_plane(m, k)
+        for m, k in active:
+            to_plane(m, k)
         for task in work.pop(t, []):
             task()
     for t in sorted(work):
         for task in work[t]:
             task()
 
-    def last(b, carry):
-        attend(passes - 1, b)
+    def last(i, carry):
+        attend(passes - 1, 2 * i)
         return carry
 
-    lax.fori_loop(0, own, last, 0)
+    lax.fori_loop(0, own // 2, last, 0)
+    join()
 
     residual = (tok_ref[...].astype(F32) + matmul(att[...], wo_x[...])).astype(BF16).astype(F32)
     second = rms_norm(residual, gain2_ref[...]).astype(BF16)
@@ -340,7 +371,7 @@
     weights[3].wait()
     out_ref[...] = (residual + matmul(hidden, down_w[...])).astype(BF16)
 
-    for m, k in ticks:
+    for m, k in [(m, k) for m in range(passes) for k in range(9)]:
         for h in range(PIECES):
             for up in (True, False):
                 if k > 0 and in_ring(k, h, up):
@@ -391,12 +422,14 @@
             pltpu.VMEM((width, 4 * LANES), BF16),
             pltpu.VMEM((2 * LANES, width), BF16),
             pltpu.VMEM((own, 2, HEADS * BLOCK, LANES), BF16),
-            pltpu.VMEM((keys, 4 * LANES), BF16),
-            pltpu.VMEM((HEADS * BLOCK, keys), F32),
-            pltpu.VMEM((HEADS * BLOCK, keys), BF16),
-            pltpu.VMEM((own, 2, BLOCK, LANES), F32),
-            pltpu.VMEM((own, 2, BLOCK, 128), F32),
+            pltpu.VMEM((passes, 2, count, LANES), F32),
+            pltpu.VMEM((passes, 2, count, 128), F32),
             pltpu.VMEM((count, 2 * LANES), BF16),
+        ]
+        + [pltpu.VMEM((keys, 4 * LANES), BF16)] * 2
+        + [pltpu.VMEM((HEADS * BLOCK, keys), F32)] * 4
+        + [pltpu.VMEM((HEADS * BLOCK, keys), BF16)] * 4
+        + [
             pltpu.VMEM((NJ, 1, 128), jnp.int32),
             pltpu.VMEM((NJ, 1, 128), jnp.int32),
             pltpu.SMEM((NJ, 1, 128), jnp.int32),

time: 125 us -> 113 us (0.904)
  Pallas kernels: 123 us -> 111 us
    pallas_call x1, Pallas kernels: 123 us -> 111 us  [body(): pl.pallas_call(fused_kernel, name='block', out_shape=jax.ShapeDtypeStruct...]
where the time goes in v3:
time: 113 us; the launch traced here: 112 us
  Pallas kernels  111 us (98%)
  local copies, waits for them, and re-layouts  1.78 us (2%)
    pallas_call x1, Pallas kernels, body(): pl.pallas_call(fused_kernel, name='block', out_shape=jax.ShapeDtypeStruct...  111 us

profile of v3, /device:TPU:1, one launch (start us, length us, event | category | flops | bytes accessed | tf_op | source)
XLA Modules:
  0.0 112.4 jit_solution(13694035615053752082)
XLA Ops:
  0.0 110.6 %block.1 = bf16[512,384]{1,0:T(8,128)(2,1)} custom-call(s32[8,20]{1,0:T(8,128)} %kb_ref.1, s32[128]{0:T(128)} %counts_ref.1, bf16[512,384]{1,0:T(8,128)(2,1)} %tok_ref.1, f32[384]{0:T(512)} %gain_ref.1, f32[384]{0:T(512)} %gain2_ref.1, bf16[384,1152]{1,0:T(8,128)(2,1)} %qkv_any.1, bf16[384,384]{1,0:T(8,128)(2,1)} %wo_any.1, bf16[384,1536]{1,0:T(8,128)(2,1)} %up_any.1, ...), custom_call_target="tpu_custom_call" | custom-call | tf_op jit(solution)/shard_map/block/pallas_call | solution.py:402
  110.6 1.8 %copy.11 = bf16[512,384]{1,0:T(8,128)(2,1)} copy(bf16[512,384]{1,0:T(8,128)(2,1)} %block.1) | data formatting | bytes 786432

commit v4 on v3

--- a/solution.py
+++ b/solution.py
@@ -19,7 +19,7 @@
 SPARE = 192
 ROWS = (32, 32)
 LAG = 2
-PIECES = 2
+PIECES = 1
 MESH = pl.DeviceIdType.MESH
 F32, BF16 = jnp.float32, jnp.bfloat16
 
@@ -130,8 +130,8 @@
             recv_sem=(fr_sem if up else br_sem).at[m, k, h],
             device_id=(z_up if up else z_down, x), device_id_type=MESH)
 
-    def in_ring(k, h, up):
-        return k < 8 or (k == 8 and (h < PIECES // 2) == up)
+    def in_ring(m, k, h, up):
+        return k < 8 or (k == 8 and (m % 2 == 1) == up)
 
     def near_copy(o):
         return pltpu.make_async_remote_copy(
@@ -345,9 +345,9 @@
                 continue
             for h in range(PIECES):
                 for up in (True, False):
-                    if in_ring(k, h, up):
+                    if in_ring(m, k, h, up):
                         ring(m, k, h, up).wait_recv()
-                        if in_ring(k + 1, h, up):
+                        if in_ring(m, k + 1, h, up):
                             ring(m, k + 1, h, up).start()
         for m, k in active:
             to_plane(m, k)
@@ -367,14 +367,17 @@
     residual = (tok_ref[...].astype(F32) + matmul(att[...], wo_x[...])).astype(BF16).astype(F32)
     second = rms_norm(residual, gain2_ref[...]).astype(BF16)
     weights[2].wait()
-    hidden = jax.nn.gelu(matmul(second, up_w[...])).astype(BF16)
     weights[3].wait()
-    out_ref[...] = (residual + matmul(hidden, down_w[...])).astype(BF16)
+    result = residual
+    for c in range(0, up_w.shape[1], 512):
+        hidden = jax.nn.gelu(matmul(second, up_w[:, c:c + 512])).astype(BF16)
+        result = result + matmul(hidden, down_w[c:c + 512])
+    out_ref[...] = result.astype(BF16)
 
     for m, k in [(m, k) for m in range(passes) for k in range(9)]:
         for h in range(PIECES):
             for up in (True, False):
-                if k > 0 and in_ring(k, h, up):
+                if k > 0 and in_ring(m, k, h, up):
                     ring(m, k, h, up).wait_send()
         plane_copy(m, k, 1, NJ - 1).wait_send()
     for o in range(1, NX):

time: 113 us -> 112 us (level)
  no operation moved by 1% of the time
where the time goes in v4:
time: 112 us
  Pallas kernels  110 us (98%)
  local copies, waits for them, and re-layouts  1.78 us (2%)
    pallas_call x1, Pallas kernels, body(): pl.pallas_call(fused_kernel, name='block', out_shape=jax.ShapeDtypeStruct...  110 us

profile of v4, /device:TPU:1, one launch (start us, length us, event | category | flops | bytes accessed | tf_op | source)
XLA Modules:
  0.0 111.8 jit_solution(12155991678748973452)
XLA Ops:
  0.0 110.0 %block.1 = bf16[512,384]{1,0:T(8,128)(2,1)} custom-call(s32[8,20]{1,0:T(8,128)} %kb_ref.1, s32[128]{0:T(128)} %counts_ref.1, bf16[512,384]{1,0:T(8,128)(2,1)} %tok_ref.1, f32[384]{0:T(512)} %gain_ref.1, f32[384]{0:T(512)} %gain2_ref.1, bf16[384,1152]{1,0:T(8,128)(2,1)} %qkv_any.1, bf16[384,384]{1,0:T(8,128)(2,1)} %wo_any.1, bf16[384,1536]{1,0:T(8,128)(2,1)} %up_any.1, ...), custom_call_target="tpu_custom_call" | custom-call | tf_op jit(solution)/shard_map/block/pallas_call | solution.py:405
  110.0 1.8 %copy.11 = bf16[512,384]{1,0:T(8,128)(2,1)} copy(bf16[512,384]{1,0:T(8,128)(2,1)} %block.1) | data formatting | bytes 786432
